TPU v7x, 512 devices: a whole 4x8x8 slice. The times are simulated.
512 devices in a mesh: req: 64 (over x, y, core), kv: 8 (over z).
Axes of the slice: x: 4, y: 8, z: 8, core: 2. Of those that a mesh axis runs over, the one named last changes fastest.
Arguments:
- tokens: bfloat16 [64, 4096], P('req'), may hold values from -6 to 6
- attn_gain: float32 [4096], replicated, may hold values from 0.5 to 1.5
- mlp_gain: float32 [4096], replicated, may hold values from 0.5 to 1.5
- w_query: bfloat16 [4096, 4096], P('req', 'kv'), may hold values from -0.09375 to 0.09375
- w_key: bfloat16 [4096, 1024], P('req', 'kv'), may hold values from -0.09375 to 0.09375
- w_value: bfloat16 [4096, 1024], P('req', 'kv'), may hold values from -0.09375 to 0.09375
- w_out: bfloat16 [4096, 4096], P('kv', 'req'), may hold values from -0.09375 to 0.09375
- w_gate: bfloat16 [4096, 14336], P('kv', 'req'), may hold values from -0.09375 to 0.09375
- w_up: bfloat16 [4096, 14336], P('kv', 'req'), may hold values from -0.09375 to 0.09375
- w_down: bfloat16 [14336, 4096], P('req', 'kv'), may hold values from -0.046875 to 0.046875
- cache_keys: bfloat16 [1024, 256, 1024], P('req', None, 'kv')
- cache_values: bfloat16 [1024, 256, 1024], P('req', None, 'kv'), may hold values from -6 to 6
- slot_owner: int32 [1024], P('req'), may hold values from 0 to 63, as said below
- slot_fill: int32 [1024], P('req'), may hold values from 0 to 256, as said below
Outputs:
- out: bfloat16 [64, 4096], P('req', 'kv')
Inputs may be any that keep to these rules, and one draw needn't show every extreme that they name: `slot_owner`: every request owns one slot or more. `slot_fill`: every index of req holds one full slot and one empty slot.
All inputs are finite; a program needn't handle non-finite values.
Results may differ from a plain program's by a relative error of at most 0.013.
The roundings to bfloat16 on the way count: a program that leaves them out, or rounds other values in their place, can miss the bound.
Values may be sent and summed in bfloat16 or wider, within the bound.
A program may use at most 64 MiB of HBM per device.

v0:
```python
import jax
import jax.numpy as jnp
from jax import lax
from jax.sharding import PartitionSpec as P

HQ = 32
HK = 8
DH = 128


EPS = 1e-05
NEG = -1e30


def joined_2(array, axis, combine):
    everything = jax.tree.map(lambda part: lax.all_gather(part, axis), array)
    initial = jax.tree.map(lambda part: part[0], everything)

    def step(k, so_far):
        return combine(so_far, jax.tree.map(lambda part: part[k], everything))

    return lax.fori_loop(1, lax.axis_size(axis), step, initial)


def rms_norm(rows, gain):
    mean = jnp.mean(rows * rows, axis=-1, keepdims=True)
    return (rows * lax.rsqrt(mean + EPS) * gain).astype(jnp.bfloat16)


def combine_parts(first, second):
    highest = jnp.maximum(first[0], second[0])
    left = jnp.exp(first[0] - highest)
    right = jnp.exp(second[0] - highest)
    return (
        highest,
        first[1] * left + second[1] * right,
        first[2] * left[..., None] + second[2] * right[..., None],
    )


def finish_heads(run_max, run_total, run_acc, query, new_key, new_value, scale):
    own_score = (
        jnp.sum(query.astype(jnp.float32) * new_key.astype(jnp.float32)[:, :, None, :], axis=-1)
        * scale
    )
    highest = jnp.maximum(run_max, own_score)
    older = jnp.exp(run_max - highest)
    fresh = jnp.exp(own_score - highest)
    total = run_total * older + fresh
    accum = (
        run_acc * older[..., None] + fresh[..., None] * new_value.astype(jnp.float32)[:, :, None, :]
    )
    return (accum / total[..., None]).astype(jnp.bfloat16).reshape(query.shape[0], -1)


def per_device(
    tokens,
    attn_gain,
    mlp_gain,
    w_query,
    w_key,
    w_value,
    w_out,
    w_gate,
    w_up,
    w_down,
    cache_keys,
    cache_values,
    slot_owner,
    slot_fill,
):
    req_count = lax.axis_size("req")
    kv_count = lax.axis_size("kv")
    local_rows = tokens.shape[0]
    requests = local_rows * req_count
    group = HQ // HK
    kv_local = cache_keys.shape[2] // DH
    scale = DH ** (-0.5)
    resid_in = tokens.astype(jnp.float32)
    normed = rms_norm(resid_in, attn_gain)
    feature_cols = lax.all_to_all(normed, "req", split_axis=1, concat_axis=0, tiled=True)
    joined = jnp.concatenate([w_query, w_key, w_value], axis=1)
    width_q = w_query.shape[1]
    width_k = w_key.shape[1]
    partial_proj = jnp.dot(feature_cols, joined, preferred_element_type=jnp.float32)
    projected = lax.psum(partial_proj, "req").astype(jnp.bfloat16)
    query = projected[:, :width_q].reshape(requests, kv_local, group, DH)
    new_key = projected[:, width_q : width_q + width_k].reshape(requests, kv_local, DH)
    new_value = projected[:, width_q + width_k :].reshape(requests, kv_local, DH)
    slots = cache_keys.shape[0]
    block_len = cache_keys.shape[1]
    keys_four = cache_keys.reshape(slots, block_len, kv_local, DH)
    values_four = cache_values.reshape(slots, block_len, kv_local, DH)
    slot_query = jnp.take(query, slot_owner, axis=0)
    scores = (
        jnp.einsum("skgd,sbkd->skgb", slot_query, keys_four, preferred_element_type=jnp.float32)
        * scale
    )
    valid = (lax.broadcasted_iota(jnp.int32, (slots, block_len), 1) < slot_fill[:, None])[
        :, None, None, :
    ]
    masked = jnp.where(valid, scores, NEG)
    slot_max = jnp.max(masked, axis=-1)
    prob = jnp.where(valid, jnp.exp(masked - slot_max[..., None]), 0.0)
    slot_total = jnp.sum(prob, axis=-1)
    slot_acc = jnp.einsum(
        "skgb,sbkd->skgd",
        prob.astype(jnp.bfloat16),
        values_four,
        preferred_element_type=jnp.float32,
    )
    run_max = jnp.full((requests, kv_local, group), NEG, jnp.float32).at[slot_owner].max(slot_max)
    rescale = jnp.exp(slot_max - run_max[slot_owner])
    run_total = (
        jnp.zeros((requests, kv_local, group), jnp.float32).at[slot_owner].add(slot_total * rescale)
    )
    run_acc = (
        jnp.zeros((requests, kv_local, group, DH), jnp.float32)
        .at[slot_owner]
        .add(slot_acc * rescale[..., None])
    )
    merged_max, merged_total, merged_acc = joined_2(
        (run_max, run_total, run_acc), "req", combine_parts
    )
    heads = finish_heads(merged_max, merged_total, merged_acc, query, new_key, new_value, scale)
    out_part = jnp.dot(heads, w_out, preferred_element_type=jnp.float32)
    head_total = lax.psum(out_part, "kv")
    attn_rows = lax.all_to_all(head_total, "req", split_axis=0, concat_axis=1, tiled=True)
    resid = resid_in + attn_rows
    normed2 = rms_norm(resid, mlp_gain)
    feature_width = normed2.shape[1] // kv_count
    kv_start = lax.axis_index("kv") * feature_width
    feature_block = lax.dynamic_slice_in_dim(normed2, kv_start, feature_width, 1)
    gate_up = jnp.concatenate([w_gate, w_up], axis=1)
    both_parts = jnp.dot(
        lax.all_gather(feature_block, "req", axis=0, tiled=True),
        gate_up,
        preferred_element_type=jnp.float32,
    )
    both_sums = lax.psum_scatter(
        both_parts.astype(jnp.bfloat16), "kv", scatter_dimension=0, tiled=True
    ).astype(jnp.float32)
    hidden_width = w_gate.shape[1]
    hidden = (jax.nn.silu(both_sums[:, :hidden_width]) * both_sums[:, hidden_width:]).astype(
        jnp.bfloat16
    )
    down_parts = jnp.dot(
        lax.all_gather(hidden, "kv", axis=0, tiled=True), w_down, preferred_element_type=jnp.float32
    )
    down_home = lax.psum_scatter(down_parts, "req", scatter_dimension=0, tiled=True)
    resid_block = lax.dynamic_slice_in_dim(resid, kv_start, feature_width, 1)
    return (resid_block + down_home).astype(jnp.bfloat16)


def solution(mesh):
    placed = (
        P("req", None),
        P(),
        P(),
        P("req", "kv"),
        P("req", "kv"),
        P("req", "kv"),
        P("kv", "req"),
        P("kv", "req"),
        P("kv", "req"),
        P("req", "kv"),
        P("req", None, "kv"),
        P("req", None, "kv"),
        P("req"),
        P("req"),
    )
    return jax.shard_map(
        per_device, mesh=mesh, in_specs=placed, out_specs=P("req", "kv"), check_vma=False
    )
```

profile of v0, /device:TPU:1, one launch (start us, length us, event | category | flops | bytes accessed | tf_op | source)
XLA Modules:
  0.0 840.2 jit_solution(18141316335080766035)
XLA Ops:
  6.6 1.5 multiply_reduce_fusion.2
  10.2 11.6 %all-to-all-start = ((bf16[1,64,64]{2,0,1:T(2,128)(2,1)}), bf16[1,64,64]{2,0,1:T(2,128)(2,1)S(1)}, u32[]{:S(2)}, u32[]{:S(2)}) async-start(bf16[1,64,64]{2,0,1:T(2,128)(2,1)} %all_to_all.30), calls=%async_computation | async-start | bytes 65536 | tf_op jit(solution)/shard_map/all_to_all | solution.py:81
  23.9 7.2 all-to-all-done
  32.2 241.8 %all-reduce.5 = bf16[64,768]{1,0:T(8,128)(2,1)S(1)} all-reduce(f32[64,768]{1,0:T(8,128)S(1)} %fusion.10), channel_id=1, replica_groups=mesh['req'=64,'kv'=8] {'req'}, use_global_device_ids=true, to_apply=%region_1.0 | all-reduce | flops 49152 | bytes 294912 | tf_op jit(solution)/shard_map/psum | solution.py:86
  276.4 1.5 convolution_multiply_fusion.1
  281.0 52.1 %all-gather.4 = f32[64,64,4]{1,2,0:T(4,128)S(1)} all-gather(f32[1,64,4]{1,2,0:T(4,128)S(1)} %copy.60), channel_id=3, replica_groups=mesh['req'=64,'kv'=8] {'req'}, dimensions={0}, use_global_device_ids=true | all-gather | bytes 66560 | tf_op jit(solution)/shard_map/all_gather | solution.py:16
  333.1 50.0 %all-gather.3 = f32[64,64,4]{1,2,0:T(4,128)S(1)} all-gather(f32[1,64,4]{1,2,0:T(4,128)S(1)} %copy.59), channel_id=2, replica_groups=mesh['req'=64,'kv'=8] {'req'}, dimensions={0}, use_global_device_ids=true | all-gather | bytes 66560 | tf_op jit(solution)/shard_map/all_gather | solution.py:16
  384.0 100.0 %while.19 = (s32[]{:T(128)}, f32[64,1,4]{0,2,1:T(4,128)S(1)}, f32[64,1,4]{0,2,1:T(4,128)S(1)}, f32[64,1,4,128]{3,2,1,0:T(4,128)S(1)}, f32[64,64,1,4]{1,3,2,0:T(4...) while((s32[]{:T(128)}, f32[64,1,4]{0,2,1:T(4,128)S(1)}, ...), condition=%wide.region_8.9_spmd, body=%wide.region_7.8_spmd.sunk | while | flops 100101 | bytes 412819 | solution.py:22
  384.3 1.3 fusion.60
  385.9 1.3 fusion.60
  387.5 1.3 fusion.60
  389.1 1.3 fusion.60
  390.6 1.3 fusion.60
  392.2 1.3 fusion.60
  393.8 1.3 fusion.60
  484.7 29.5 %psum.15 = f32[64,1,64]{2,0,1:T(8,128)} all-reduce(f32[64,1,64]{2,0,1:T(8,128)S(1)} %convolution_bitcast_fusion), channel_id=1, replica_groups=mesh['req'=64,'kv'=8] {'kv'}, use_global_device_ids=true, to_apply=%region_10.11 | all-reduce | flops 4096 | bytes 32768 | tf_op jit(solution)/shard_map/psum | solution.py:127
  514.3 11.5 %all-to-all-start.1 = ((f32[64,1,64]{2,1,0:T(1,128)}), f32[64,1,64]{2,1,0:T(1,128)S(1)}, u32[]{:S(2)}, u32[]{:S(2)}) async-start(f32[64,1,64]{2,1,0:T(1,128)} %bitcast.23), calls=%async_computation.1 | async-start | bytes 65536 | tf_op jit(solution)/shard_map/all_to_all | solution.py:128
  525.9 9.3 %all-to-all-done.1 = f32[64,1,64]{2,1,0:T(1,128)S(1)} async-done(((f32[64,1,64]{2,1,0:T(1,128)}), f32[64,1,64]{2,1,0:T(1,128)S(1)}, u32[]{:S(2)}, u32[]{:S(2)}) %all-to-all-start.1) | async-done | bytes 16416 | tf_op jit(solution)/shard_map/all_to_all | solution.py:128
  538.5 48.1 %all-gather.5 = bf16[64,1,512]{2,1,0:T(2,128)(2,1)S(1)} all-gather(bf16[1,1,512]{2,1,0:T(2,128)(2,1)S(1)} %fusion.40), channel_id=1, replica_groups=mesh['req'=64,'kv'=8] {'req'}, dimensions={0}, use_global_device_ids=true | all-gather | bytes 66560 | tf_op jit(solution)/shard_map/all_gather | solution.py:136
  587.6 26.7 %reduce-scatter.2.cloned.1.call-done = bf16[8,448]{1,0:T(8,128)(2,1)} async-done(((bf16[64,448]{1,0:T(8,128)(2,1)}), bf16[8,448]{1,0:T(8,128)(2,1)}) %reduce-scatter.2.cloned.1.call-update) | async-done | bytes 7184 | tf_op jit(solution)/shard_map/reduce_scatter | solution.py:140
  615.0 18.3 %all_gather.31 = bf16[64,224]{1,0:T(8,128)(2,1)S(1)} all-gather(bf16[8,224]{1,0:T(8,128)(2,1)S(1)} %fusion.34), channel_id=1, replica_groups=mesh['req'=64,'kv'=8] {'kv'}, dimensions={0}, use_global_device_ids=true | all-gather | bytes 32256 | tf_op jit(solution)/shard_map/all_gather | solution.py:148
  634.2 1.3 dynamic-slice
  635.5 196.2 %all-reduce.4.cloned.1.call-done = f32[64,512]{1,0:T(8,128)} async-done(((f32[64,512]{1,0:T(8,128)}), f32[64,512]{1,0:T(8,128)}) %all-reduce.4.cloned.1.call-update) | async-done | bytes 131088
  831.7 1.9 fusion.41
  (435 shorter events, 105.4 us)
Async XLA Ops:
  6.5 268.1 %copy-start = (bf16[16,256,128]{2,1,0:T(8,128)(2,1)S(1)}, bf16[16,256,128]{2,1,0:T(8,128)(2,1)}, u32[]{:S(2)}) copy-start(bf16[16,256,128]{2,1,0:T(8,128)(2,1)} %param.26) | copy-start | bytes 3145732
  6.5 529.9 %copy-start.3 = (bf16[1,4096]{1,0:T(2,128)(2,1)S(1)}, bf16[1,4096]{1,0:T(2,128)(2,1)}, u32[]{:S(2)}) copy-start(bf16[1,4096]{1,0:T(2,128)(2,1)} %param.16) | copy-start | bytes 24580
  6.5 478.1 %copy-start.4 = (bf16[512,64]{0,1:T(8,128)(2,1)S(1)}, bf16[512,64]{0,1:T(8,128)(2,1)}, u32[]{:S(2)}) copy-start(bf16[512,64]{0,1:T(8,128)(2,1)} %param.22) | copy-start | bytes 196612
  6.5 580.0 %copy-start.5 = (bf16[512,224]{0,1:T(8,128)(2,1)S(1)}, bf16[512,224]{0,1:T(8,128)(2,1)}, u32[]{:S(2)}) copy-start(bf16[512,224]{0,1:T(8,128)(2,1)} %param.24) | copy-start | bytes 688132
  6.5 580.0 %copy-start.6 = (bf16[512,224]{0,1:T(8,128)(2,1)S(1)}, bf16[512,224]{0,1:T(8,128)(2,1)}, u32[]{:S(2)}) copy-start(bf16[512,224]{0,1:T(8,128)(2,1)} %param.23) | copy-start | bytes 688132
  6.5 626.8 %copy-start.2 = (bf16[224,512]{1,0:T(8,128)(2,1)S(1)}, bf16[224,512]{1,0:T(8,128)(2,1)}, u32[]{:S(2)}) copy-start(bf16[224,512]{1,0:T(8,128)(2,1)} %param.25) | copy-start | bytes 688132
  10.2 20.9 %all-to-all-start = ((bf16[1,64,64]{2,0,1:T(2,128)(2,1)}), bf16[1,64,64]{2,0,1:T(2,128)(2,1)S(1)}, u32[]{:S(2)}, u32[]{:S(2)}) async-start(bf16[1,64,64]{2,0,1:T(2,128)(2,1)} %all_to_all.30), calls=%async_computation | async-start | bytes 65536 | tf_op jit(solution)/shard_map/all_to_all | solution.py:81
  21.8 361.3 %all-gather.8.cloned.1.call-start = ((), (), s32[]{:S(2)}) async-start(), calls=%async_computation.4 | async-start | bytes 8519680 | tf_op jit(solution)/shard_map/all_gather | solution.py:16
  279.0 0.7 copy-start.1
  514.3 20.8 %all-to-all-start.1 = ((f32[64,1,64]{2,1,0:T(1,128)}), f32[64,1,64]{2,1,0:T(1,128)S(1)}, u32[]{:S(2)}, u32[]{:S(2)}) async-start(f32[64,1,64]{2,1,0:T(1,128)} %bitcast.23), calls=%async_computation.1 | async-start | bytes 65536 | tf_op jit(solution)/shard_map/all_to_all | solution.py:128
  525.8 88.5 %reduce-scatter.2.cloned.1.call-start = ((), (), s32[]{:S(2)}) async-start(), calls=%async_computation.3 | async-start | bytes 73728 | tf_op jit(solution)/shard_map/reduce_scatter | solution.py:140
  587.5 244.2 %all-reduce.4.cloned.1.call-start = ((), (), s32[]{:S(2)}) async-start(), calls=%async_computation.5 | async-start | bytes 262144
Sparse Core Ops, SparseCore 0:
  279.8 90.5 all-gather.7
  587.6 26.5 reduce-scatter.1
  634.3 197.3 all-reduce.3
where the time goes:
time: 842 us; the launch traced here: 840 us
  blocking collectives  440 us (52%)
  waiting for transfers between devices  239 us (28%)
  other arithmetic  97.7 us (12%)
  starting transfers between devices  23.2 us (3%)
  local copies, waits for them, and re-layouts  18.2 us (2%)
  between operations  14.7 us (2%)
    psum x1, blocking collectives, per_device(): projected = lax.psum(partial_proj, 'req').astype(jnp.bfloat16)  242 us
    unnamed x4, waiting for transfers between devices  196 us
    all_gather x2, blocking collectives, joined_2(): everything = jax.tree.map(lambda part: lax.all_gather(part, axis), array)  102 us
    add x63, other arithmetic, combine_parts(): first[2] * left[..., None] + second[2] * right[..., None]  83.3 us
    all_gather x1, blocking collectives, per_device(): lax.all_gather(feature_block, 'req', axis=0, tiled=True)  48.1 us
    psum x1, blocking collectives, per_device(): head_total = lax.psum(out_part, 'kv')  29.5 us
    reduce_scatter x1, waiting for transfers between devices, per_device(): lax.psum_scatter(both_parts.astype(jnp.bfloat16), 'kv', scatter_dimension...  26.7 us
    all_gather x1, blocking collectives, per_device(): lax.all_gather(hidden, 'kv', axis=0, tiled=True)  18.3 us
  transfers between devices with their start and end apart: 5, of which 4 were waited for; matrix products, arithmetic and copies ran while one was open for 1% of the time, Pallas kernels for 0%

commit v1 on v0

--- a/solution.py
+++ b/solution.py
@@ -12,14 +12,17 @@
 NEG = -1e30
 
 
-def joined_2(array, axis, combine):
-    everything = jax.tree.map(lambda part: lax.all_gather(part, axis), array)
-    initial = jax.tree.map(lambda part: part[0], everything)
+def scatter_sum(rows, axis):
+    parts = lax.all_to_all(rows, axis, split_axis=0, concat_axis=0, tiled=True)
+    devices = lax.axis_size(axis)
+    return jnp.sum(parts.reshape((devices, -1) + parts.shape[1:]), axis=0)
 
-    def step(k, so_far):
-        return combine(so_far, jax.tree.map(lambda part: part[k], everything))
 
-    return lax.fori_loop(1, lax.axis_size(axis), step, initial)
+def spread(row, axis):
+    devices = lax.axis_size(axis)
+    copies = jnp.broadcast_to(row[None], (devices,) + row.shape)
+    parts = lax.all_to_all(copies, axis, split_axis=0, concat_axis=0, tiled=True)
+    return parts.reshape((devices * row.shape[0],) + row.shape[1:])
 
 
 def rms_norm(rows, gain):
@@ -27,15 +30,13 @@
     return (rows * lax.rsqrt(mean + EPS) * gain).astype(jnp.bfloat16)
 
 
-def combine_parts(first, second):
-    highest = jnp.maximum(first[0], second[0])
-    left = jnp.exp(first[0] - highest)
-    right = jnp.exp(second[0] - highest)
-    return (
-        highest,
-        first[1] * left + second[1] * right,
-        first[2] * left[..., None] + second[2] * right[..., None],
-    )
+def merge_parts(parts, group):
+    acc = parts[:, : group * DH].reshape(-1, group, DH)
+    part_max = parts[:, group * DH : group * DH + group]
+    part_total = parts[:, group * DH + group : group * DH + 2 * group]
+    highest = jnp.max(part_max, axis=0)
+    share = jnp.exp(part_max - highest)
+    return highest, jnp.sum(part_total * share, axis=0), jnp.sum(acc * share[..., None], axis=0)
 
 
 def finish_heads(run_max, run_total, run_acc, query, new_key, new_value, scale):
@@ -83,10 +84,11 @@
     width_q = w_query.shape[1]
     width_k = w_key.shape[1]
     partial_proj = jnp.dot(feature_cols, joined, preferred_element_type=jnp.float32)
-    projected = lax.psum(partial_proj, "req").astype(jnp.bfloat16)
-    query = projected[:, :width_q].reshape(requests, kv_local, group, DH)
-    new_key = projected[:, width_q : width_q + width_k].reshape(requests, kv_local, DH)
-    new_value = projected[:, width_q + width_k :].reshape(requests, kv_local, DH)
+    projected = scatter_sum(partial_proj, "req").astype(jnp.bfloat16)
+    own_query = projected[:, :width_q]
+    new_key = projected[:, width_q : width_q + width_k].reshape(local_rows, kv_local, DH)
+    new_value = projected[:, width_q + width_k :].reshape(local_rows, kv_local, DH)
+    query = spread(own_query, "req").reshape(requests, kv_local, group, DH)
     slots = cache_keys.shape[0]
     block_len = cache_keys.shape[1]
     keys_four = cache_keys.reshape(slots, block_len, kv_local, DH)
@@ -119,13 +121,30 @@
         .at[slot_owner]
         .add(slot_acc * rescale[..., None])
     )
-    merged_max, merged_total, merged_acc = joined_2(
-        (run_max, run_total, run_acc), "req", combine_parts
+    packed = jnp.concatenate(
+        [
+            run_acc.reshape(requests, group * DH),
+            run_max.reshape(requests, group),
+            run_total.reshape(requests, group),
+            jnp.zeros((requests, DH - 2 * group), jnp.float32),
+        ],
+        axis=1,
     )
-    heads = finish_heads(merged_max, merged_total, merged_acc, query, new_key, new_value, scale)
+    parts = lax.all_to_all(packed, "req", split_axis=0, concat_axis=0, tiled=True)
+    merged_max, merged_total, merged_acc = merge_parts(parts, group)
+    own_heads = finish_heads(
+        merged_max[None, None],
+        merged_total[None, None],
+        merged_acc[None, None],
+        own_query.reshape(local_rows, kv_local, group, DH),
+        new_key,
+        new_value,
+        scale,
+    )
+    heads = spread(own_heads, "req")
     out_part = jnp.dot(heads, w_out, preferred_element_type=jnp.float32)
-    head_total = lax.psum(out_part, "kv")
-    attn_rows = lax.all_to_all(head_total, "req", split_axis=0, concat_axis=1, tiled=True)
+    attn_part = lax.all_to_all(out_part, "req", split_axis=0, concat_axis=1, tiled=True)
+    attn_rows = jnp.sum(spread(attn_part, "kv"), axis=0, keepdims=True)
     resid = resid_in + attn_rows
     normed2 = rms_norm(resid, mlp_gain)
     feature_width = normed2.shape[1] // kv_count
@@ -133,21 +152,24 @@
     feature_block = lax.dynamic_slice_in_dim(normed2, kv_start, feature_width, 1)
     gate_up = jnp.concatenate([w_gate, w_up], axis=1)
     both_parts = jnp.dot(
-        lax.all_gather(feature_block, "req", axis=0, tiled=True),
+        spread(feature_block, "req"),
         gate_up,
         preferred_element_type=jnp.float32,
     )
-    both_sums = lax.psum_scatter(
-        both_parts.astype(jnp.bfloat16), "kv", scatter_dimension=0, tiled=True
-    ).astype(jnp.float32)
+    both_sums = lax.all_to_all(
+        both_parts.astype(jnp.bfloat16), "kv", split_axis=0, concat_axis=0, tiled=True
+    )
+    both_sums = jnp.sum(
+        both_sums.reshape(kv_count, requests // kv_count, -1).astype(jnp.float32), axis=0
+    )
     hidden_width = w_gate.shape[1]
     hidden = (jax.nn.silu(both_sums[:, :hidden_width]) * both_sums[:, hidden_width:]).astype(
         jnp.bfloat16
     )
     down_parts = jnp.dot(
-        lax.all_gather(hidden, "kv", axis=0, tiled=True), w_down, preferred_element_type=jnp.float32
+        spread(hidden, "kv"), w_down, preferred_element_type=jnp.float32
     )
-    down_home = lax.psum_scatter(down_parts, "req", scatter_dimension=0, tiled=True)
+    down_home = scatter_sum(down_parts, "req")
     resid_block = lax.dynamic_slice_in_dim(resid, kv_start, feature_width, 1)
     return (resid_block + down_home).astype(jnp.bfloat16)
 

time: 842 us -> 188 us (0.22)
  blocking collectives: 440 us -> 99.9 us
  waiting for transfers between devices: 239 us -> 38.3 us
  other arithmetic: 97.7 us -> 12.1 us
  between operations: 14.7 us -> 1.79 us
  local copies, waits for them, and re-layouts: 18.2 us -> 7.94 us
    psum x2 -> x0, blocking collectives: 271 us -> none  [the longest x1 242 us: per_device(): projected = lax.psum(partial_proj, 'req').astype(jnp.bfloat16)]
    unnamed x4 -> x0, waiting for transfers between devices: 196 us -> none
    all_gather x4 -> x0, blocking collectives: 168 us -> none  [the longest x2 102 us: joined_2(): everything = jax.tree.map(lambda part: lax.all_gather(part, axis), array)]
    all_to_all x0 -> x7, blocking collectives: none -> 99.9 us  [the longest x3 39.7 us: spread(): lax.all_to_all(copies, axis, split_axis=0, concat_axis=0, tiled=True)]
    add x63 -> x1, other arithmetic: 83.3 us -> 0.01 us  [finish_heads(): total = run_total * older + fresh]
    reduce_scatter x1 -> x0, waiting for transfers between devices: 26.7 us -> none  [per_device(): lax.psum_scatter(both_parts.astype(jnp.bfloat16), 'kv', scatter_dimension...]
    all_to_all x2 -> x4, waiting for transfers between devices: 16.5 us -> 38.3 us  [the longest x2 17.4 us: spread(): lax.all_to_all(copies, axis, split_axis=0, concat_axis=0, tiled=True)]
    mul x126 -> x1, local copies, waits for them, and re-layouts: 12.1 us -> 0.12 us  [merge_parts(): acc * share[..., None]]
  transfers between devices with their start and end apart: 5 -> 4, of which waited for: 4 -> 4; matrix products, arithmetic and copies ran while one was open for 1% -> 0% of each run, Pallas kernels for 0% -> 0%
where the time goes in v1:
time: 188 us; the launch traced here: 187 us
  blocking collectives  99.9 us (53%)
  waiting for transfers between devices  38.3 us (20%)
  starting transfers between devices  25.1 us (13%)
  other arithmetic  12.1 us (6%)
  local copies, waits for them, and re-layouts  7.94 us (4%)
    all_to_all x3, blocking collectives, spread(): lax.all_to_all(copies, axis, split_axis=0, concat_axis=0, tiled=True)  39.7 us
    all_to_all x1, blocking collectives, per_device(): lax.all_to_all(normed, 'req', split_axis=1, concat_axis=0, tiled=True)  20.9 us
    all_to_all x2, waiting for transfers between devices, spread(): lax.all_to_all(copies, axis, split_axis=0, concat_axis=0, tiled=True)  17.4 us
    all_to_all x1, blocking collectives, scatter_sum(): parts = lax.all_to_all(rows, axis, split_axis=0, concat_axis=0, tiled=True)  16.5 us
    all_to_all x2, starting transfers between devices, spread(): lax.all_to_all(copies, axis, split_axis=0, concat_axis=0, tiled=True)  15.8 us
    all_to_all x1, blocking collectives, per_device(): lax.all_to_all(out_part, 'req', split_axis=0, concat_axis=1, tiled=True)  13.2 us
    all_to_all x1, waiting for transfers between devices, per_device(): lax.all_to_all(packed, 'req', split_axis=0, concat_axis=0, tiled=True)  10.6 us
    all_to_all x1, waiting for transfers between devices, scatter_sum(): parts = lax.all_to_all(rows, axis, split_axis=0, concat_axis=0, tiled=True)  10.3 us
  transfers between devices with their start and end apart: 4, of which 4 were waited for; matrix products, arithmetic and copies ran while one was open for 0% of the time, Pallas kernels for 0%

profile of v1, /device:TPU:1, one launch (start us, length us, event | category | flops | bytes accessed | tf_op | source)
XLA Modules:
  0.0 186.6 jit_solution(17087683935578873897)
XLA Ops:
  0.0 1.5 multiply_reduce_fusion.1
  2.2 0.8 convert_reduce_fusion.1
  3.1 20.9 %all_to_all.94 = bf16[1,64,64]{2,0,1:T(2,128)(2,1)S(1)} all-to-all(bf16[1,64,64]{2,0,1:T(2,128)(2,1)S(1)} %all_to_all.82), channel_id=1, replica_groups=mesh['req'=64,'kv'=8] {'req'}, dimensions={1} | all-to-all | bytes 16384 | tf_op jit(solution)/shard_map/all_to_all | solution.py:82
  24.1 0.9 copy.27
  25.0 4.8 %all-to-all-start.1 = ((f32[64,1,768]{2,1,0:T(1,128)}), f32[64,1,768]{2,1,0:T(1,128)S(1)}, u32[]{:S(2)}, u32[]{:S(2)}) async-start(f32[64,1,768]{2,1,0:T(1,128)} %copy.27), calls=%async_computation.1 | async-start | bytes 393216 | tf_op jit(solution)/shard_map/all_to_all | solution.py:16
  30.6 10.3 %all-to-all-done.1 = f32[64,1,768]{2,1,0:T(1,128)S(1)} async-done(((f32[64,1,768]{2,1,0:T(1,128)}), f32[64,1,768]{2,1,0:T(1,128)S(1)}, u32[]{:S(2)}, u32[]{:S(2)}) %all-to-all-start.1) | async-done | bytes 196640 | tf_op jit(solution)/shard_map/all_to_all | solution.py:16
  41.7 1.0 reduce.26
  43.3 5.8 %all-to-all-start.2 = ((bf16[64,2,256]{2,1,0:T(2,128)(2,1)}), bf16[64,2,256]{2,1,0:T(2,128)(2,1)S(1)}, u32[]{:S(2)}, u32[]{:S(2)}) async-start(bf16[64,2,256]{2,1,0:T(2,128)(2,1)} %reshape.434), calls=%async_computation.2 | async-start | bytes 131072 | tf_op jit(solution)/shard_map/all_to_all | solution.py:24
  49.2 9.7 %all-to-all-done.2 = bf16[64,2,256]{2,1,0:T(2,128)(2,1)S(1)} async-done(((bf16[64,2,256]{2,1,0:T(2,128)(2,1)}), bf16[64,2,256]{2,1,0:T(2,128)(2,1)S(1)}, u32[]{:S(2)}, u32[]{:S(2)}) %all-to-all-start.2) | async-done | bytes 65568 | tf_op jit(solution)/shard_map/all_to_all | solution.py:24
  62.9 1.1 scatter_fusion
  64.9 4.4 %all-to-all-start.3 = ((f32[64,1,640]{2,1,0:T(1,128)}), f32[64,1,640]{2,1,0:T(1,128)S(1)}, u32[]{:S(2)}, u32[]{:S(2)}) async-start(f32[64,1,640]{2,1,0:T(1,128)} %all_to_all.69), calls=%async_computation.3 | async-start | bytes 327680 | tf_op jit(solution)/shard_map/all_to_all | solution.py:133
  69.5 10.6 %all-to-all-done.3 = f32[64,1,640]{2,1,0:T(1,128)S(1)} async-done(((f32[64,1,640]{2,1,0:T(1,128)}), f32[64,1,640]{2,1,0:T(1,128)S(1)}, u32[]{:S(2)}, u32[]{:S(2)}) %all-to-all-start.3) | async-done | bytes 163872 | tf_op jit(solution)/shard_map/all_to_all | solution.py:133
  80.7 1.0 reduce.27
  81.7 14.9 %all_to_all.95 = bf16[64,2,256]{2,1,0:T(2,128)(2,1)S(1)} all-to-all(bf16[64,2,256]{2,1,0:T(2,128)(2,1)S(1)} %reshape.436), channel_id=1, replica_groups=mesh['req'=64,'kv'=8] {'req'}, dimensions={0} | all-to-all | bytes 131072 | tf_op jit(solution)/shard_map/all_to_all | solution.py:24
  96.7 0.8 copy-done.4
  97.6 13.2 %all_to_all.96 = f32[64,1,64]{2,1,0:T(1,128)S(1)} all-to-all(f32[64,1,64]{2,1,0:T(1,128)S(1)} %bitcast.69), channel_id=1, replica_groups=mesh['req'=64,'kv'=8] {'req'}, dimensions={0} | all-to-all | bytes 32768 | tf_op jit(solution)/shard_map/all_to_all | solution.py:146
  111.4 0.8 reduce.25
  112.9 10.0 %all-to-all-start.6 = ((f32[8,1,4096]{2,1,0:T(1,128)}), f32[8,1,4096]{2,1,0:T(1,128)S(1)}, u32[]{:S(2)}, u32[]{:S(2)}) async-start(f32[8,1,4096]{2,1,0:T(1,128)} %broadcast_in_dim.121), calls=%async_computation.6 | async-start | bytes 262144 | tf_op jit(solution)/shard_map/all_to_all | solution.py:24
  123.0 7.8 %all-to-all-done.6 = f32[8,1,4096]{2,1,0:T(1,128)S(1)} async-done(((f32[8,1,4096]{2,1,0:T(1,128)}), f32[8,1,4096]{2,1,0:T(1,128)S(1)}, u32[]{:S(2)}, u32[]{:S(2)}) %all-to-all-start.6) | async-done | bytes 131104 | tf_op jit(solution)/shard_map/all_to_all | solution.py:24
  133.1 1.1 reduce.28
  134.2 15.5 %all_to_all.97 = bf16[64,2,256]{2,1,0:T(2,128)(2,1)S(1)} all-to-all(bf16[64,2,256]{2,1,0:T(2,128)(2,1)S(1)} %reshape.438), channel_id=1, replica_groups=mesh['req'=64,'kv'=8] {'req'}, dimensions={0} | all-to-all | bytes 131072 | tf_op jit(solution)/shard_map/all_to_all | solution.py:24
  150.1 9.6 %all_to_all.98 = bf16[8,8,448]{2,1,0:T(8,128)(2,1)S(1)} all-to-all(bf16[8,8,448]{2,1,0:T(8,128)(2,1)S(1)} %fusion.1), channel_id=1, replica_groups=mesh['req'=64,'kv'=8] {'kv'}, dimensions={0} | all-to-all | bytes 114688 | tf_op jit(solution)/shard_map/all_to_all | solution.py:159
  159.8 9.3 %all_to_all.99 = bf16[8,8,224]{2,1,0:T(8,128)(2,1)S(1)} all-to-all(bf16[8,8,224]{2,1,0:T(8,128)(2,1)S(1)} %broadcast_in_dim.126), channel_id=1, replica_groups=mesh['req'=64,'kv'=8] {'kv'}, dimensions={0} | all-to-all | bytes 57344 | tf_op jit(solution)/shard_map/all_to_all | solution.py:24
  169.4 16.5 %all_to_all.100 = f32[64,1,512]{2,1,0:T(1,128)S(1)} all-to-all(f32[64,1,512]{2,1,0:T(1,128)S(1)} %copy.30), channel_id=1, replica_groups=mesh['req'=64,'kv'=8] {'req'}, dimensions={0} | all-to-all | bytes 262144 | tf_op jit(solution)/shard_map/all_to_all | solution.py:16
  (85 shorter events, 12.6 us)
Async XLA Ops:
  0.0 60.0 %copy-start = (bf16[16,256,128]{2,1,0:T(8,128)(2,1)S(1)}, bf16[16,256,128]{2,1,0:T(8,128)(2,1)}, u32[]{:S(2)}) copy-start(bf16[16,256,128]{2,1,0:T(8,128)(2,1)} %param.24) | copy-start | bytes 3145732
  0.0 2.2 %copy-start.2 = (bf16[1,4096]{1,0:T(2,128)(2,1)S(1)}, bf16[1,4096]{1,0:T(2,128)(2,1)}, u32[]{:S(2)}) copy-start(bf16[1,4096]{1,0:T(2,128)(2,1)} %param.14) | copy-start | bytes 24580
  2.2 21.8 %copy-start.3 = (bf16[64,512]{1,0:T(8,128)(2,1)S(1)}, bf16[64,512]{1,0:T(8,128)(2,1)}, u32[]{:S(2)}) copy-start(bf16[64,512]{1,0:T(8,128)(2,1)} %param.17) | copy-start | bytes 196612
  3.1 20.9 %copy-start.5 = (bf16[64,128]{1,0:T(8,128)(2,1)S(1)}, bf16[64,128]{1,0:T(8,128)(2,1)}, u32[]{:S(2)}) copy-start(bf16[64,128]{1,0:T(8,128)(2,1)} %param.19) | copy-start | bytes 49156
  3.1 20.9 %copy-start.6 = (bf16[64,128]{1,0:T(8,128)(2,1)S(1)}, bf16[64,128]{1,0:T(8,128)(2,1)}, u32[]{:S(2)}) copy-start(bf16[64,128]{1,0:T(8,128)(2,1)} %param.18) | copy-start | bytes 49156
  25.0 4.9 %copy-start.11 = (s32[16]{0:T(128)S(1)}, s32[16]{0:T(128)}, u32[]{:S(2)}) copy-start(s32[16]{0:T(128)} %param.26) | copy-start | bytes 196
  25.0 15.9 %all-to-all-start.1 = ((f32[64,1,768]{2,1,0:T(1,128)}), f32[64,1,768]{2,1,0:T(1,128)S(1)}, u32[]{:S(2)}, u32[]{:S(2)}) async-start(f32[64,1,768]{2,1,0:T(1,128)} %copy.27), calls=%async_computation.1 | async-start | bytes 393216 | tf_op jit(solution)/shard_map/all_to_all | solution.py:16
  29.9 0.7 copy-start.7
  43.3 19.2 %copy-start.8 = (bf16[16,256,128]{2,1,0:T(8,128)(2,1)S(1)}, bf16[16,256,128]{2,1,0:T(8,128)(2,1)}, u32[]{:S(2)}) copy-start(bf16[16,256,128]{2,1,0:T(8,128)(2,1)} %param.25) | copy-start | bytes 3145732
  43.3 15.6 %all-to-all-start.2 = ((bf16[64,2,256]{2,1,0:T(2,128)(2,1)}), bf16[64,2,256]{2,1,0:T(2,128)(2,1)S(1)}, u32[]{:S(2)}, u32[]{:S(2)}) async-start(bf16[64,2,256]{2,1,0:T(2,128)(2,1)} %reshape.434), calls=%async_computation.2 | async-start | bytes 131072 | tf_op jit(solution)/shard_map/all_to_all | solution.py:24
  64.9 15.2 %all-to-all-start.3 = ((f32[64,1,640]{2,1,0:T(1,128)}), f32[64,1,640]{2,1,0:T(1,128)S(1)}, u32[]{:S(2)}, u32[]{:S(2)}) async-start(f32[64,1,640]{2,1,0:T(1,128)} %all_to_all.69), calls=%async_computation.3 | async-start | bytes 327680 | tf_op jit(solution)/shard_map/all_to_all | solution.py:133
  96.6 0.8 copy-start.4
  112.9 17.8 %all-to-all-start.6 = ((f32[8,1,4096]{2,1,0:T(1,128)}), f32[8,1,4096]{2,1,0:T(1,128)S(1)}, u32[]{:S(2)}, u32[]{:S(2)}) async-start(f32[8,1,4096]{2,1,0:T(1,128)} %broadcast_in_dim.121), calls=%async_computation.6 | async-start | bytes 262144 | tf_op jit(solution)/shard_map/all_to_all | solution.py:24
  133.1 16.7 %copy-start.10 = (bf16[512,224]{0,1:T(8,128)(2,1)S(1)}, bf16[512,224]{0,1:T(8,128)(2,1)}, u32[]{:S(2)}) copy-start(bf16[512,224]{0,1:T(8,128)(2,1)} %param.21) | copy-start | bytes 688132
  134.1 15.6 %copy-start.9 = (bf16[512,224]{0,1:T(8,128)(2,1)S(1)}, bf16[512,224]{0,1:T(8,128)(2,1)}, u32[]{:S(2)}) copy-start(bf16[512,224]{0,1:T(8,128)(2,1)} %param.22) | copy-start | bytes 688132
  150.0 19.1 %copy-start.1 = (bf16[224,512]{1,0:T(8,128)(2,1)S(1)}, bf16[224,512]{1,0:T(8,128)(2,1)}, u32[]{:S(2)}) copy-start(bf16[224,512]{1,0:T(8,128)(2,1)} %param.23) | copy-start | bytes 688132

commit v2 on v0

v2 whole, which is shorter than its diff:
```python
import jax
import jax.numpy as jnp
from jax import lax
from jax.experimental import pallas as pl
from jax.experimental.pallas import tpu as pltpu
from jax.sharding import PartitionSpec as P

HQ = 32
HK = 8
DH = 128
GROUP = HQ // HK
PAD = 8

EPS = 1e-05
NEG = -1e30
MESH = pl.DeviceIdType.MESH
F32 = jnp.float32
BF16 = jnp.bfloat16


def dot(left, right):
    return jnp.dot(left, right, preferred_element_type=F32)


def exchange_start(axis, me, count, source, landing, send_sem, recv_sem):
    @pl.loop(1, count)
    def _(step):
        peer = lax.rem(me + step, count)
        pltpu.make_async_remote_copy(
            src_ref=source(peer),
            dst_ref=landing.at[me],
            send_sem=send_sem,
            recv_sem=recv_sem,
            device_id={axis: peer},
            device_id_type=MESH,
        ).start()

    pltpu.make_async_copy(source(me), landing.at[me], recv_sem).start()


def landed(landing, recv_sem):
    pltpu.make_async_copy(landing, landing, recv_sem).wait()


def sent(landing, count, send_sem):
    view = landing.at[pl.ds(0, count - 1)]
    pltpu.make_async_copy(view, view, send_sem).wait()


def one_row(block):
    turned = pltpu.roll(block, 64, 1)
    low = lax.broadcasted_iota(jnp.int32, (1, 128), 1) < 64
    pairs = [
        jnp.where(low, block[2 * i : 2 * i + 1], turned[2 * i + 1 : 2 * i + 2]) for i in range(4)
    ]
    return jnp.concatenate(pairs, axis=1)


def layer_kernel(
    req_count,
    kv_count,
    owner_ref,
    fill_ref,
    tok_ref,
    again_ref,
    mgain_ref,
    wq_hbm,
    wk_hbm,
    wv_hbm,
    wo_hbm,
    wg_hbm,
    wu_hbm,
    wd_hbm,
    keys_hbm,
    values_hbm,
    out_ref,
    wq,
    wk,
    wv,
    wo,
    wg,
    wu,
    wd,
    keys,
    values,
    s1,
    l1,
    s2,
    l2,
    s3,
    l3,
    s4,
    l4,
    s5,
    l5,
    s6,
    l6,
    s7,
    l7,
    s8,
    l8,
    s9,
    l9,
    s10,
    l10,
    s11,
    l11,
    load_sem,
    send_sem,
    recv_sem,
):
    req = lax.axis_index("req")
    kv = lax.axis_index("kv")
    slots = keys.shape[0]
    block_len = keys.shape[1]
    scale = DH ** (-0.5)
    features = req_count * 64

    barrier = pltpu.get_barrier_semaphore()

    @pl.loop(1, req_count)
    def _(step):
        pl.semaphore_signal(
            barrier,
            inc=1,
            device_id={"req": lax.rem(req + step, req_count)},
            device_id_type=MESH,
        )

    @pl.loop(1, kv_count)
    def _(step):
        pl.semaphore_signal(
            barrier,
            inc=1,
            device_id={"kv": lax.rem(kv + step, kv_count)},
            device_id_type=MESH,
        )

    loads = [
        pltpu.make_async_copy(source, target, load_sem.at[i])
        for i, (source, target) in enumerate(
            [
                (wq_hbm, wq),
                (wk_hbm, wk),
                (wv_hbm, wv),
                (keys_hbm, keys),
                (values_hbm, values),
                (wo_hbm, wo),
                (wg_hbm, wg),
                (wu_hbm, wu),
                (wd_hbm, wd),
            ]
        )
    ]
    for load in loads:
        load.start()

    def req_start(i, source, landing):
        exchange_start("req", req, req_count, source, landing, send_sem.at[i], recv_sem.at[i])

    def kv_start(i, source, landing):
        exchange_start("kv", kv, kv_count, source, landing, send_sem.at[i], recv_sem.at[i])

    def kv_rows(array):
        return lambda peer: array.at[pl.ds(pl.multiple_of(peer * 8, 8), 8)]

    tok = tok_ref[...]
    mean = jnp.sum(jnp.sum(tok * tok, axis=1, keepdims=True), axis=0, keepdims=True) / features
    normed = (tok * lax.rsqrt(mean + EPS) * again_ref[...]).astype(BF16).astype(F32)
    s1[:, 0, :] = normed

    pl.semaphore_wait(barrier, req_count - 1 + kv_count - 1)

    req_start(0, lambda peer: s1.at[peer], l1)
    for load in loads[:3]:
        load.wait()
    landed(l1, recv_sem.at[0])
    columns = l1[:, 0, :][:, :64].astype(BF16)
    width_q = wq.shape[1]
    s2[:, 0, :] = jnp.concatenate(
        [dot(columns, wq[...]), dot(columns, wk[...]), dot(columns, wv[...])], axis=1
    )
    req_start(1, lambda peer: s2.at[peer], l2)
    landed(l2, recv_sem.at[1])
    projected = jnp.sum(l2[...], axis=0).astype(BF16).astype(F32)
    own_query = [projected[:, g * DH : (g + 1) * DH] for g in range(GROUP)]
    new_key = projected[:, width_q : width_q + DH]
    new_value = projected[:, width_q + DH : width_q + 2 * DH]
    for g in range(GROUP):
        s3[g : g + 1, :] = own_query[g]
    req_start(2, lambda peer: s3, l3)
    for load in loads[3:5]:
        load.wait()
    landed(l3, recv_sem.at[2])

    pos = lax.broadcasted_iota(jnp.int32, (PAD, block_len), 1)
    scores = []
    valid = []
    lane = lax.broadcasted_iota(jnp.int32, (1, slots * PAD), 1)
    slot_key = jnp.zeros((1, slots * PAD), jnp.int32)
    for s in range(slots):
        query = l3[owner_ref[s]]
        query = jnp.concatenate([query, jnp.zeros((PAD - GROUP, DH), F32)], axis=0).astype(BF16)
        scores.append(
            lax.dot_general(
                query, keys[s], (((1,), (1,)), ((), ())), preferred_element_type=F32
            )
        )
        valid.append(jnp.where(pos < fill_ref[s], 1.0, 0.0))
        slot_key = jnp.where(lane // PAD == s, owner_ref[s], slot_key)
    valid = jnp.concatenate(valid, axis=0) > 0.5
    masked = jnp.where(valid, jnp.concatenate(scores, axis=0) * scale, NEG)
    slot_max = jnp.max(masked, axis=1, keepdims=True)
    prob = jnp.where(valid, jnp.exp(masked - slot_max), 0.0)
    slot_total = jnp.sum(prob, axis=1, keepdims=True)
    prob_low = prob.astype(BF16)
    slot_acc = jnp.concatenate(
        [dot(prob_low[s * PAD : (s + 1) * PAD], values[s]) for s in range(slots)], axis=0
    )
    rows = slots * PAD
    slot_side = jnp.concatenate([slot_acc, jnp.broadcast_to(slot_total, (rows, DH))], axis=1)
    max_lane = jnp.transpose(jnp.broadcast_to(slot_max, (rows, rows)))[0:1]
    request = lax.broadcasted_iota(jnp.int32, (req_count, rows), 0)
    extra_lane = lax.broadcasted_iota(jnp.int32, (req_count, DH), 1)
    extra = jnp.zeros((req_count, DH), F32)
    for g in range(GROUP):
        mine = (request == slot_key) & (lane % PAD == g)
        part_max = jnp.max(jnp.where(mine, max_lane, NEG), axis=1, keepdims=True)
        weight = jnp.where(mine, jnp.exp(jnp.where(mine, max_lane, NEG) - part_max), 0.0)
        part = jnp.dot(
            weight, slot_side, preferred_element_type=F32, precision=lax.Precision.HIGHEST
        )
        s4[:, 0, g * DH : (g + 1) * DH] = part[:, :DH]
        extra = jnp.where(extra_lane == 2 * g, part[:, DH:], extra)
        extra = jnp.where(extra_lane == 2 * g + 1, part_max, extra)
    s4[:, 0, GROUP * DH :] = extra
    req_start(3, lambda peer: s4.at[peer], l4)
    landed(l4, recv_sem.at[3])

    extra = l4[:, 0, GROUP * DH :]
    for g in range(GROUP):
        part_total = extra[:, 2 * g : 2 * g + 1]
        part_max = extra[:, 2 * g + 1 : 2 * g + 2]
        run_max = jnp.max(part_max, axis=0, keepdims=True)
        share = jnp.exp(part_max - run_max)
        run_total = jnp.sum(part_total * share, axis=0, keepdims=True)
        run_acc = jnp.sum(l4[:, 0, g * DH : (g + 1) * DH] * share, axis=0, keepdims=True)
        own_score = jnp.sum(own_query[g] * new_key, axis=1, keepdims=True) * scale
        highest = jnp.maximum(run_max, own_score)
        older = jnp.exp(run_max - highest)
        fresh = jnp.exp(own_score - highest)
        total = run_total * older + fresh
        heads = (run_acc * older + fresh * new_value) / total
        s5[:, g * DH : (g + 1) * DH] = heads.astype(BF16).astype(F32)
    req_start(4, lambda peer: s5, l5)
    loads[5].wait()
    landed(l5, recv_sem.at[4])

    out_part = dot(l5[:, 0, :].astype(BF16), wo[...])
    s6[:, 0, :] = jnp.concatenate([out_part, jnp.zeros((req_count, 64), F32)], axis=1)
    req_start(5, lambda peer: s6.at[peer], l6)
    landed(l6, recv_sem.at[5])
    s7[...] = l6[:, 0, :]
    kv_start(6, kv_rows(s7), l7)
    landed(l7, recv_sem.at[6])
    block = pl.ds(pl.multiple_of(kv * 8, 8), 8)
    resid = tok_ref[block, :] + jnp.sum(l7[...], axis=0)
    squares = jnp.sum(jnp.sum(resid * resid, axis=1, keepdims=True), axis=0, keepdims=True)
    resid_row = one_row(resid)
    s8[:, :512] = one_row(resid * mgain_ref[block, :])
    s8[:, 512:] = jnp.broadcast_to(squares, (1, 128))
    req_start(7, lambda peer: s8, l8)
    for load in loads[6:8]:
        load.wait()
    landed(l8, recv_sem.at[7])

    scaled = l8[:, 0, :512].astype(BF16)
    width = wg.shape[1]
    s9[:, 128:256] = l8[:, 0, 512:]
    s9[:, :width] = dot(scaled, wg[...])
    s9[:, 384:512] = jnp.zeros((req_count, 128), F32)
    s9[:, 256 : 256 + width] = dot(scaled, wu[...])
    kv_start(8, kv_rows(s9), l9)
    landed(l9, recv_sem.at[8])
    both = jnp.sum(l9[...], axis=0)
    factor = lax.rsqrt(both[:, 255:256] / features + EPS)
    gate = both[:, :256] * factor
    up = both[:, 256:] * factor
    hidden = (gate / (1.0 + jnp.exp(-gate)) * up).astype(BF16).astype(F32)
    s10[...] = hidden
    kv_start(9, lambda peer: s10, l10)
    loads[8].wait()
    landed(l10, recv_sem.at[9])
    units = l10[...].reshape(req_count, 256)[:, :width].astype(BF16)
    s11[:, 0, :] = dot(units, wd[...])
    req_start(10, lambda peer: s11.at[peer], l11)
    landed(l11, recv_sem.at[10])
    out_ref[...] = (resid_row + jnp.sum(l11[...], axis=0)).astype(BF16)

    for i, landing in enumerate([l1, l2, l3, l4, l5, l6, l7, l8, l9, l10, l11]):
        sent(landing, landing.shape[0], send_sem.at[i])


def per_device(
    tokens,
    attn_gain,
    mlp_gain,
    w_query,
    w_key,
    w_value,
    w_out,
    w_gate,
    w_up,
    w_down,
    cache_keys,
    cache_values,
    slot_owner,
    slot_fill,
):
    n = lax.axis_size("req")
    m = lax.axis_size("kv")

    def padded(row):
        return jnp.pad(row.astype(F32).reshape(n, 64), ((0, 0), (0, 64)))

    smem = pl.BlockSpec(memory_space=pltpu.SMEM)
    vmem = pl.BlockSpec(memory_space=pltpu.VMEM)
    anywhere = pl.BlockSpec(memory_space=pl.ANY)
    stored = [w_query, w_key, w_value, w_out, w_gate, w_up, w_down, cache_keys, cache_values]
    pairs = [
        ((n, 1, 128), (n, 1, 128)),
        ((n, 1, 768), (n, 1, 768)),
        ((4, 128), (n, 4, 128)),
        ((n, 1, 640), (n, 1, 640)),
        ((1, 512), (n, 1, 512)),
        ((n, 1, 128), (n, 1, 128)),
        ((n, 128), (m, 8, 128)),
        ((1, 640), (n, 1, 640)),
        ((n, 512), (m, 8, 512)),
        ((8, 256), (m, 8, 256)),
        ((n, 1, 512), (n, 1, 512)),
    ]

    def kernel(*refs):
        layer_kernel(n, m, *refs)

    return pl.pallas_call(
        kernel,
        out_shape=jax.ShapeDtypeStruct((1, 512), BF16),
        in_specs=[smem, smem, vmem, vmem, vmem] + [anywhere] * len(stored),
        out_specs=vmem,
        scratch_shapes=[pltpu.VMEM(array.shape, array.dtype) for array in stored]
        + [pltpu.VMEM(shape, F32) for pair in pairs for shape in pair]
        + [
            pltpu.SemaphoreType.DMA((len(stored),)),
            pltpu.SemaphoreType.DMA((len(pairs),)),
            pltpu.SemaphoreType.DMA((len(pairs),)),
        ],
        compiler_params=pltpu.CompilerParams(
            collective_id=0, has_side_effects=True, vmem_limit_bytes=32 << 20
        ),
        name="decode_layer",
    )(
        slot_owner,
        slot_fill,
        padded(tokens),
        padded(attn_gain),
        padded(mlp_gain),
        *stored,
    )


def solution(mesh):
    placed = (
        P("req", None),
        P(),
        P(),
        P("req", "kv"),
        P("req", "kv"),
        P("req", "kv"),
        P("kv", "req"),
        P("kv", "req"),
        P("kv", "req"),
        P("req", "kv"),
        P("req", None, "kv"),
        P("req", None, "kv"),
        P("req"),
        P("req"),
    )
    return jax.shard_map(
        per_device, mesh=mesh, in_specs=placed, out_specs=P("req", "kv"), check_vma=False
    )
```

time: 842 us -> 101 us (0.12)
  blocking collectives: 440 us -> 0 us
  waiting for transfers between devices: 239 us -> 0 us
  other arithmetic: 97.7 us -> 0.86 us
  Pallas kernels: 0 us -> 93 us
  starting transfers between devices: 23.2 us -> 0 us
  between operations: 14.7 us -> 0.15 us
  local copies, waits for them, and re-layouts: 18.2 us -> 6.75 us
    psum x2 -> x0, blocking collectives: 271 us -> none  [the longest x1 242 us: per_device(): projected = lax.psum(partial_proj, 'req').astype(jnp.bfloat16)]
    unnamed x4 -> x0, waiting for transfers between devices: 196 us -> none
    all_gather x4 -> x0, blocking collectives: 168 us -> none  [the longest x2 102 us: joined_2(): everything = jax.tree.map(lambda part: lax.all_gather(part, axis), array)]
    pallas_call x0 -> x1, Pallas kernels: none -> 93 us  [per_device(): pl.pallas_call(kernel, out_shape=jax.ShapeDtypeStruct((1, 512), BF16), in...]
    add x63 -> x0, other arithmetic: 83.3 us -> none  [combine_parts(): first[2] * left[..., None] + second[2] * right[..., None]]
    reduce_scatter x1 -> x0, waiting for transfers between devices: 26.7 us -> none  [per_device(): lax.psum_scatter(both_parts.astype(jnp.bfloat16), 'kv', scatter_dimension...]
    all_to_all x2 -> x0, starting transfers between devices: 23.1 us -> none  [the longest x1 11.6 us: per_device(): lax.all_to_all(normed, 'req', split_axis=1, concat_axis=0, tiled=True)]
    all_to_all x2 -> x0, waiting for transfers between devices: 16.5 us -> none  [the longest x1 9.26 us: per_device(): lax.all_to_all(head_total, 'req', split_axis=0, concat_axis=1, tiled=True)]
  transfers between devices with their start and end apart: 5 -> 0, of which waited for: 4 -> 0; matrix products, arithmetic and copies ran while one was open for 1% -> 0% of each run, Pallas kernels for 0% -> 0%
where the time goes in v2:
time: 101 us
  Pallas kernels  93 us (92%)
  local copies, waits for them, and re-layouts  6.75 us (7%)
    pallas_call x1, Pallas kernels, per_device(): pl.pallas_call(kernel, out_shape=jax.ShapeDtypeStruct((1, 512), BF16), in...  93 us
    unnamed x20, local copies, waits for them, and re-layouts  5.07 us

profile of v2, /device:TPU:1, one launch (start us, length us, event | category | flops | bytes accessed | tf_op | source)
XLA Modules:
  0.0 100.8 jit_solution(46851181752392847)
XLA Ops:
  0.0 0.9 reduce
  0.9 0.1 reshape.10
  1.0 0.8 reshape.11
  1.8 0.8 reshape.12
  2.5 1.0 copy.15.refs_8_
  3.5 1.1 %copy.16.refs_9_ = bf16[512,224]{1,0:T(8,128)(2,1)S(1)} copy(bf16[512,224]{0,1:T(8,128)(2,1)} %param.21) | data formatting | bytes 458752 | tf_op args[7]
  4.6 0.0 copy-start.2
  4.6 0.0 copy-start.3
  4.6 0.0 copy-start.4
  4.6 0.0 copy-start.5
  4.6 0.0 copy-start.6
  4.7 0.0 copy-start.7
  4.7 1.2 %copy.17.refs_10_ = bf16[512,224]{1,0:T(8,128)(2,1)S(1)} copy(bf16[512,224]{0,1:T(8,128)(2,1)} %param.22) | data formatting | bytes 458752 | tf_op args[8]
  5.9 0.0 copy-done
  5.9 0.0 copy-done.2
  5.9 0.0 copy-done.3
  5.9 0.0 copy-done.4
  5.9 0.0 copy-done.5
  5.9 0.0 copy-done.6
  5.9 0.0 copy-done.7
  5.9 0.0 copy-start.1
  6.0 1.2 %copy-done.1 = bf16[16,256,128]{2,1,0:T(8,128)(2,1)S(1)} copy-done((bf16[16,256,128]{2,1,0:T(8,128)(2,1)S(1)}, bf16[16,256,128]{2,1,0:T(8,128)(2,1)}, u32[]{:S(2)}) %copy-start.1) | copy-done | bytes 1048600
  7.2 93.0 %decode_layer.1 = bf16[1,512]{1,0:T(2,128)(2,1)S(1)} custom-call(s32[16]{0:T(128)S(1)} %copy-done.6, s32[16]{0:T(128)S(1)} %copy-done.7, f32[64,128]{1,0:T(8,128)S(1)} %pad_convert_fusion.refs_2_, f32[64,128]{1,0:T(8,128)S(1)} %pad.14.refs_3_, f32[64,128]{1,0:T(8,128)S(1)} %pad.15.refs_4_, bf16[64,512]{1,0:T(8,128)(2,1)S(1)} %copy-done.3, ...), custom_call_target="tpu_custom_call" | custom-call | tf_op jit(solution)/shard_map/decode_layer/pallas_call | solution.py:347
  100.2 0.6 copy.19
  (4 shorter events, 0.0 us)
Async XLA Ops:
  0.0 5.9 %copy-start = (bf16[16,256,128]{2,1,0:T(8,128)(2,1)S(1)}, bf16[16,256,128]{2,1,0:T(8,128)(2,1)}, u32[]{:S(2)}) copy-start(bf16[16,256,128]{2,1,0:T(8,128)(2,1)} %refs_12_.1) | copy-start | bytes 3145732
  4.6 1.3 %copy-start.2 = (bf16[224,512]{1,0:T(8,128)(2,1)S(1)}, bf16[224,512]{1,0:T(8,128)(2,1)}, u32[]{:S(2)}) copy-start(bf16[224,512]{1,0:T(8,128)(2,1)} %refs_11_.1) | copy-start | bytes 688132
  4.6 1.3 %copy-start.3 = (bf16[64,512]{1,0:T(8,128)(2,1)S(1)}, bf16[64,512]{1,0:T(8,128)(2,1)}, u32[]{:S(2)}) copy-start(bf16[64,512]{1,0:T(8,128)(2,1)} %refs_5_.1) | copy-start | bytes 196612
  4.6 1.3 %copy-start.4 = (bf16[64,128]{1,0:T(8,128)(2,1)S(1)}, bf16[64,128]{1,0:T(8,128)(2,1)}, u32[]{:S(2)}) copy-start(bf16[64,128]{1,0:T(8,128)(2,1)} %refs_6_.1) | copy-start | bytes 49156
  4.6 1.3 %copy-start.5 = (bf16[64,128]{1,0:T(8,128)(2,1)S(1)}, bf16[64,128]{1,0:T(8,128)(2,1)}, u32[]{:S(2)}) copy-start(bf16[64,128]{1,0:T(8,128)(2,1)} %refs_7_.1) | copy-start | bytes 49156
  4.6 1.3 %copy-start.6 = (s32[16]{0:T(128)S(1)}, s32[16]{0:T(128)}, u32[]{:S(2)}) copy-start(s32[16]{0:T(128)} %refs_0_.1) | copy-start | bytes 196
  4.7 1.3 %copy-start.7 = (s32[16]{0:T(128)S(1)}, s32[16]{0:T(128)}, u32[]{:S(2)}) copy-start(s32[16]{0:T(128)} %refs_1_.1) | copy-start | bytes 196
  5.9 1.2 %copy-start.1 = (bf16[16,256,128]{2,1,0:T(8,128)(2,1)S(1)}, bf16[16,256,128]{2,1,0:T(8,128)(2,1)}, u32[]{:S(2)}) copy-start(bf16[16,256,128]{2,1,0:T(8,128)(2,1)} %refs_13_.1) | copy-start | bytes 3145732

commit v3 on v2

--- a/solution.py
+++ b/solution.py
@@ -23,9 +23,9 @@
 
 
 def exchange_start(axis, me, count, source, landing, send_sem, recv_sem):
-    @pl.loop(1, count)
+    @pl.loop(1, count, unroll=7)
     def _(step):
-        peer = lax.rem(me + step, count)
+        peer = lax.rem(me + count - step, count)
         pltpu.make_async_remote_copy(
             src_ref=source(peer),
             dst_ref=landing.at[me],
@@ -47,13 +47,12 @@
     pltpu.make_async_copy(view, view, send_sem).wait()
 
 
+def dot_stored(left, right):
+    return lax.dot_general(left, right, (((1,), (1,)), ((), ())), preferred_element_type=F32)
+
+
 def one_row(block):
-    turned = pltpu.roll(block, 64, 1)
-    low = lax.broadcasted_iota(jnp.int32, (1, 128), 1) < 64
-    pairs = [
-        jnp.where(low, block[2 * i : 2 * i + 1], turned[2 * i + 1 : 2 * i + 2]) for i in range(4)
-    ]
-    return jnp.concatenate(pairs, axis=1)
+    return jnp.concatenate([block[i] for i in range(block.shape[0])], axis=1)
 
 
 def layer_kernel(
@@ -165,17 +164,18 @@
         return lambda peer: array.at[pl.ds(pl.multiple_of(peer * 8, 8), 8)]
 
     tok = tok_ref[...]
-    mean = jnp.sum(jnp.sum(tok * tok, axis=1, keepdims=True), axis=0, keepdims=True) / features
-    normed = (tok * lax.rsqrt(mean + EPS) * again_ref[...]).astype(BF16).astype(F32)
-    s1[:, 0, :] = normed
+    mean = jnp.sum(jnp.sum(tok * tok, axis=0), axis=1, keepdims=True) / features
+    s1[...] = (tok * lax.rsqrt(mean + EPS) * again_ref[...]).astype(BF16).astype(F32)
+    odd = jnp.full((1, 128), lax.rem(req, 2), jnp.int32) == 1
 
     pl.semaphore_wait(barrier, req_count - 1 + kv_count - 1)
 
-    req_start(0, lambda peer: s1.at[peer], l1)
+    req_start(0, lambda peer: s1.at[peer // 2], l1)
     for load in loads[:3]:
         load.wait()
     landed(l1, recv_sem.at[0])
-    columns = l1[:, 0, :][:, :64].astype(BF16)
+    columns = l1[:, 0, :]
+    columns = jnp.where(odd, pltpu.roll(columns, 64, 1), columns)[:, :64].astype(BF16)
     width_q = wq.shape[1]
     s2[:, 0, :] = jnp.concatenate(
         [dot(columns, wq[...]), dot(columns, wk[...]), dot(columns, wv[...])], axis=1
@@ -186,8 +186,7 @@
     own_query = [projected[:, g * DH : (g + 1) * DH] for g in range(GROUP)]
     new_key = projected[:, width_q : width_q + DH]
     new_value = projected[:, width_q + DH : width_q + 2 * DH]
-    for g in range(GROUP):
-        s3[g : g + 1, :] = own_query[g]
+    s3[...] = jnp.concatenate(own_query, axis=0).astype(BF16)
     req_start(2, lambda peer: s3, l3)
     for load in loads[3:5]:
         load.wait()
@@ -199,13 +198,9 @@
     lane = lax.broadcasted_iota(jnp.int32, (1, slots * PAD), 1)
     slot_key = jnp.zeros((1, slots * PAD), jnp.int32)
     for s in range(slots):
-        query = l3[owner_ref[s]]
+        query = l3[owner_ref[s]].astype(F32)
         query = jnp.concatenate([query, jnp.zeros((PAD - GROUP, DH), F32)], axis=0).astype(BF16)
-        scores.append(
-            lax.dot_general(
-                query, keys[s], (((1,), (1,)), ((), ())), preferred_element_type=F32
-            )
-        )
+        scores.append(dot_stored(query, keys[s]))
         valid.append(jnp.where(pos < fill_ref[s], 1.0, 0.0))
         slot_key = jnp.where(lane // PAD == s, owner_ref[s], slot_key)
     valid = jnp.concatenate(valid, axis=0) > 0.5
@@ -238,6 +233,7 @@
     landed(l4, recv_sem.at[3])
 
     extra = l4[:, 0, GROUP * DH :]
+    own_heads = []
     for g in range(GROUP):
         part_total = extra[:, 2 * g : 2 * g + 1]
         part_max = extra[:, 2 * g + 1 : 2 * g + 2]
@@ -251,23 +247,27 @@
         fresh = jnp.exp(own_score - highest)
         total = run_total * older + fresh
         heads = (run_acc * older + fresh * new_value) / total
-        s5[:, g * DH : (g + 1) * DH] = heads.astype(BF16).astype(F32)
+        own_heads.append(heads)
+    s5[...] = jnp.concatenate(own_heads, axis=0).astype(BF16)
     req_start(4, lambda peer: s5, l5)
     loads[5].wait()
     landed(l5, recv_sem.at[4])
 
-    out_part = dot(l5[:, 0, :].astype(BF16), wo[...])
-    s6[:, 0, :] = jnp.concatenate([out_part, jnp.zeros((req_count, 64), F32)], axis=1)
+    every = l5[...].astype(F32)
+    every = jnp.concatenate([every[:, g, :] for g in range(GROUP)], axis=1).astype(BF16)
+    out_part = jnp.concatenate([dot_stored(every, wo[...]), jnp.zeros((req_count, 64), F32)], axis=1)
+    s6[:, 0, :] = jnp.where(odd, pltpu.roll(out_part, 64, 1), out_part)
     req_start(5, lambda peer: s6.at[peer], l6)
     landed(l6, recv_sem.at[5])
-    s7[...] = l6[:, 0, :]
-    kv_start(6, kv_rows(s7), l7)
+    both = l6[...].reshape(req_count // 2, 2, 1, 128)
+    s7[...] = both[:, 0] + both[:, 1]
+    kv_start(6, lambda peer: s7.at[pl.ds(peer * 4, 4)], l7)
     landed(l7, recv_sem.at[6])
-    block = pl.ds(pl.multiple_of(kv * 8, 8), 8)
-    resid = tok_ref[block, :] + jnp.sum(l7[...], axis=0)
-    squares = jnp.sum(jnp.sum(resid * resid, axis=1, keepdims=True), axis=0, keepdims=True)
+    block = pl.ds(kv * 4, 4)
+    resid = tok_ref[block] + jnp.sum(l7[...], axis=0)
+    squares = jnp.sum(jnp.sum(resid * resid, axis=0), axis=1, keepdims=True)
     resid_row = one_row(resid)
-    s8[:, :512] = one_row(resid * mgain_ref[block, :])
+    s8[:, :512] = one_row(resid * mgain_ref[block])
     s8[:, 512:] = jnp.broadcast_to(squares, (1, 128))
     req_start(7, lambda peer: s8, l8)
     for load in loads[6:8]:
@@ -275,11 +275,11 @@
     landed(l8, recv_sem.at[7])
 
     scaled = l8[:, 0, :512].astype(BF16)
-    width = wg.shape[1]
+    width = wg.shape[0]
     s9[:, 128:256] = l8[:, 0, 512:]
-    s9[:, :width] = dot(scaled, wg[...])
+    s9[:, :width] = dot_stored(scaled, wg[...])
     s9[:, 384:512] = jnp.zeros((req_count, 128), F32)
-    s9[:, 256 : 256 + width] = dot(scaled, wu[...])
+    s9[:, 256 : 256 + width] = dot_stored(scaled, wu[...])
     kv_start(8, kv_rows(s9), l9)
     landed(l9, recv_sem.at[8])
     both = jnp.sum(l9[...], axis=0)
@@ -320,21 +320,21 @@
     n = lax.axis_size("req")
     m = lax.axis_size("kv")
 
-    def padded(row):
-        return jnp.pad(row.astype(F32).reshape(n, 64), ((0, 0), (0, 64)))
+    def in_rows(row):
+        return row.astype(F32).reshape(n // 2, 1, 128)
 
     smem = pl.BlockSpec(memory_space=pltpu.SMEM)
     vmem = pl.BlockSpec(memory_space=pltpu.VMEM)
     anywhere = pl.BlockSpec(memory_space=pl.ANY)
-    stored = [w_query, w_key, w_value, w_out, w_gate, w_up, w_down, cache_keys, cache_values]
+    stored = [w_query, w_key, w_value, w_out.T, w_gate.T, w_up.T, w_down, cache_keys, cache_values]
     pairs = [
-        ((n, 1, 128), (n, 1, 128)),
+        ((n // 2, 1, 128), (n, 1, 128)),
         ((n, 1, 768), (n, 1, 768)),
         ((4, 128), (n, 4, 128)),
         ((n, 1, 640), (n, 1, 640)),
-        ((1, 512), (n, 1, 512)),
+        ((4, 128), (n, 4, 128)),
         ((n, 1, 128), (n, 1, 128)),
-        ((n, 128), (m, 8, 128)),
+        ((n // 2, 1, 128), (m, 4, 1, 128)),
         ((1, 640), (n, 1, 640)),
         ((n, 512), (m, 8, 512)),
         ((8, 256), (m, 8, 256)),
@@ -350,22 +350,22 @@
         in_specs=[smem, smem, vmem, vmem, vmem] + [anywhere] * len(stored),
         out_specs=vmem,
         scratch_shapes=[pltpu.VMEM(array.shape, array.dtype) for array in stored]
-        + [pltpu.VMEM(shape, F32) for pair in pairs for shape in pair]
+        + [pltpu.VMEM(s, BF16 if s[-2:] == (4, 128) else F32) for pair in pairs for s in pair]
         + [
             pltpu.SemaphoreType.DMA((len(stored),)),
             pltpu.SemaphoreType.DMA((len(pairs),)),
             pltpu.SemaphoreType.DMA((len(pairs),)),
         ],
         compiler_params=pltpu.CompilerParams(
-            collective_id=0, has_side_effects=True, vmem_limit_bytes=32 << 20
+            collective_id=0, has_side_effects=True
         ),
         name="decode_layer",
     )(
         slot_owner,
         slot_fill,
-        padded(tokens),
-        padded(attn_gain),
-        padded(mlp_gain),
+        in_rows(tokens),
+        in_rows(attn_gain),
+        in_rows(mlp_gain),
         *stored,
     )
 

time: 101 us -> 92.7 us (0.918)
  local copies, waits for them, and re-layouts: 6.75 us -> 1.25 us
  Pallas kernels: 93 us -> 89.8 us
    unnamed x20 -> x1, local copies, waits for them, and re-layouts: 5.07 us -> 1.25 us
    pallas_call x1, Pallas kernels: 93 us -> 89.8 us  [per_device(): pl.pallas_call(kernel, out_shape=jax.ShapeDtypeStruct((1, 512), BF16), in...]
    reshape x3 -> x0, local copies, waits for them, and re-layouts: 1.66 us -> none  [padded(): return jnp.pad(row.astype(F32).reshape(n, 64), ((0, 0), (0, 64)))]
    reshape x0 -> x1, other arithmetic: none -> 1.33 us  [in_rows(): return row.astype(F32).reshape(n // 2, 1, 128)]
where the time goes in v3:
time: 92.7 us; the launch traced here: 92.4 us
  Pallas kernels  89.8 us (97%)
  other arithmetic  1.33 us (1%)
  local copies, waits for them, and re-layouts  1.25 us (1%)
    pallas_call x1, Pallas kernels, per_device(): pl.pallas_call(kernel, out_shape=jax.ShapeDtypeStruct((1, 512), BF16), in...  89.8 us

profile of v3, /device:TPU:1, one launch (start us, length us, event | category | flops | bytes accessed | tf_op | source)
XLA Modules:
  0.0 92.4 jit_solution(11732557370650778542)
XLA Ops:
  0.0 1.3 %bitcast_convert_fusion.refs_2_ = f32[32,1,128]{2,1,0:T(1,128)} fusion(bf16[1,4096]{1,0:T(2,128)(2,1)} %param.14), kind=kLoop, calls=%fused_computation | loop fusion | flops 4096 | bytes 24576 | tf_op jit(solution)/shard_map/reshape | solution.py:324
  1.3 89.8 %decode_layer.1 = bf16[1,512]{1,0:T(2,128)(2,1)} custom-call(s32[16]{0:T(128)} %refs_0_.1, s32[16]{0:T(128)} %refs_1_.1, f32[32,1,128]{2,1,0:T(1,128)} %bitcast_convert_fusion.refs_2_, f32[32,1,128]{2,1,0:T(1,128)} %bitcast.11, f32[32,1,128]{2,1,0:T(1,128)} %bitcast.12, bf16[64,512]{1,0:T(8,128)(2,1)} %refs_5_.1, bf16[64,128]{1,0:T(8,128)(2,1)} %refs_6_.1, ...), custom_call_target="tpu_custom_call" | custom-call | tf_op jit(solution)/shard_map/decode_layer/pallas_call | solution.py:347
  91.1 1.3 %copy.16 = bf16[1,512]{1,0:T(2,128)(2,1)} copy(bf16[1,512]{1,0:T(2,128)(2,1)} %decode_layer.1) | data formatting | bytes 2048

commit v4 on v3

--- a/solution.py
+++ b/solution.py
@@ -104,6 +104,7 @@
     l10,
     s11,
     l11,
+    t9,
     load_sem,
     send_sem,
     recv_sem,
@@ -117,7 +118,7 @@
 
     barrier = pltpu.get_barrier_semaphore()
 
-    @pl.loop(1, req_count)
+    @pl.loop(1, req_count, unroll=7)
     def _(step):
         pl.semaphore_signal(
             barrier,
@@ -159,9 +160,6 @@
 
     def kv_start(i, source, landing):
         exchange_start("kv", kv, kv_count, source, landing, send_sem.at[i], recv_sem.at[i])
-
-    def kv_rows(array):
-        return lambda peer: array.at[pl.ds(pl.multiple_of(peer * 8, 8), 8)]
 
     tok = tok_ref[...]
     mean = jnp.sum(jnp.sum(tok * tok, axis=0), axis=1, keepdims=True) / features
@@ -265,37 +263,47 @@
     landed(l7, recv_sem.at[6])
     block = pl.ds(kv * 4, 4)
     resid = tok_ref[block] + jnp.sum(l7[...], axis=0)
-    squares = jnp.sum(jnp.sum(resid * resid, axis=0), axis=1, keepdims=True)
     resid_row = one_row(resid)
-    s8[:, :512] = one_row(resid * mgain_ref[block])
-    s8[:, 512:] = jnp.broadcast_to(squares, (1, 128))
+    gained = resid * mgain_ref[block]
+    s8[...] = jnp.concatenate([gained[i] for i in range(4)], axis=0).astype(BF16)
+    inverse = one_row(1.0 / mgain_ref[block])
     req_start(7, lambda peer: s8, l8)
     for load in loads[6:8]:
         load.wait()
     landed(l8, recv_sem.at[7])
 
-    scaled = l8[:, 0, :512].astype(BF16)
+    every = l8[...].astype(F32)
+    every = jnp.concatenate([every[:, i, :] for i in range(4)], axis=1)
+    scaled = every.astype(BF16)
+    plain = every * inverse
+    squares = jnp.sum(plain * plain, axis=1, keepdims=True)
+    high = squares.astype(BF16).astype(F32)
+    first = lax.broadcasted_iota(jnp.int32, (req_count, 128), 1) < 112
     width = wg.shape[0]
-    s9[:, 128:256] = l8[:, 0, 512:]
-    s9[:, :width] = dot_stored(scaled, wg[...])
-    s9[:, 384:512] = jnp.zeros((req_count, 128), F32)
-    s9[:, 256 : 256 + width] = dot_stored(scaled, wu[...])
-    kv_start(8, kv_rows(s9), l9)
+    t9[:, 128:256] = jnp.where(first, high, squares - high)
+    t9[:, :width] = dot_stored(scaled, wg[...])
+    t9[:, 384:512] = jnp.zeros((req_count, 128), F32)
+    t9[:, 256 : 256 + width] = dot_stored(scaled, wu[...])
+    s9[...] = t9[...].reshape(kv_count, 8, 512).astype(BF16)
+    kv_start(8, lambda peer: s9.at[peer], l9)
     landed(l9, recv_sem.at[8])
-    both = jnp.sum(l9[...], axis=0)
-    factor = lax.rsqrt(both[:, 255:256] / features + EPS)
+    both = jnp.sum(l9[...].astype(F32), axis=0)
+    squares = both[:, 224:225] + both[:, 255:256]
+    factor = lax.rsqrt(squares / features + EPS)
     gate = both[:, :256] * factor
     up = both[:, 256:] * factor
-    hidden = (gate / (1.0 + jnp.exp(-gate)) * up).astype(BF16).astype(F32)
-    s10[...] = hidden
+    s10[...] = (gate / (1.0 + jnp.exp(-gate)) * up).astype(BF16)
     kv_start(9, lambda peer: s10, l10)
     loads[8].wait()
     landed(l10, recv_sem.at[9])
-    units = l10[...].reshape(req_count, 256)[:, :width].astype(BF16)
-    s11[:, 0, :] = dot(units, wd[...])
+    units = l10[...].astype(F32).reshape(req_count, 256)[:, :width].astype(BF16)
+    down = dot(units, wd[...])
+    s11[...] = jnp.stack([down[:, i * 128 : (i + 1) * 128] for i in range(4)], axis=1).astype(BF16)
     req_start(10, lambda peer: s11.at[peer], l11)
     landed(l11, recv_sem.at[10])
-    out_ref[...] = (resid_row + jnp.sum(l11[...], axis=0)).astype(BF16)
+    down = jnp.sum(l11[...].astype(F32), axis=0)
+    down = jnp.concatenate([down[i : i + 1] for i in range(4)], axis=1)
+    out_ref[...] = (resid_row + down).astype(BF16)
 
     for i, landing in enumerate([l1, l2, l3, l4, l5, l6, l7, l8, l9, l10, l11]):
         sent(landing, landing.shape[0], send_sem.at[i])
@@ -335,11 +343,13 @@
         ((4, 128), (n, 4, 128)),
         ((n, 1, 128), (n, 1, 128)),
         ((n // 2, 1, 128), (m, 4, 1, 128)),
-        ((1, 640), (n, 1, 640)),
-        ((n, 512), (m, 8, 512)),
+        ((4, 128), (n, 4, 128)),
+        ((m, 8, 512), (m, 8, 512)),
         ((8, 256), (m, 8, 256)),
-        ((n, 1, 512), (n, 1, 512)),
+        ((n, 4, 128), (n, 4, 128)),
     ]
+
+    low = ((4, 128), (8, 512), (8, 256))
 
     def kernel(*refs):
         layer_kernel(n, m, *refs)
@@ -350,8 +360,9 @@
         in_specs=[smem, smem, vmem, vmem, vmem] + [anywhere] * len(stored),
         out_specs=vmem,
         scratch_shapes=[pltpu.VMEM(array.shape, array.dtype) for array in stored]
-        + [pltpu.VMEM(s, BF16 if s[-2:] == (4, 128) else F32) for pair in pairs for s in pair]
+        + [pltpu.VMEM(s, BF16 if s[-2:] in low else F32) for pair in pairs for s in pair]
         + [
+            pltpu.VMEM((n, 512), F32),
             pltpu.SemaphoreType.DMA((len(stored),)),
             pltpu.SemaphoreType.DMA((len(pairs),)),
             pltpu.SemaphoreType.DMA((len(pairs),)),

time: 92.7 us -> 90.4 us (0.975)
  Pallas kernels: 89.8 us -> 87.5 us
    pallas_call x1, Pallas kernels: 89.8 us -> 87.5 us  [per_device(): pl.pallas_call(kernel, out_shape=jax.ShapeDtypeStruct((1, 512), BF16), in...]
where the time goes in v4:
time: 90.4 us; the launch traced here: 90.1 us
  Pallas kernels  87.5 us (97%)
  other arithmetic  1.33 us (1%)
  local copies, waits for them, and re-layouts  1.25 us (1%)
    pallas_call x1, Pallas kernels, per_device(): pl.pallas_call(kernel, out_shape=jax.ShapeDtypeStruct((1, 512), BF16), in...  87.5 us

profile of v4, /device:TPU:1, one launch (start us, length us, event | category | flops | bytes accessed | tf_op | source)
XLA Modules:
  0.0 90.1 jit_solution(12660138455072957122)
XLA Ops:
  0.0 1.3 %bitcast_convert_fusion.refs_2_ = f32[32,1,128]{2,1,0:T(1,128)} fusion(bf16[1,4096]{1,0:T(2,128)(2,1)} %param.14), kind=kLoop, calls=%fused_computation | loop fusion | flops 4096 | bytes 24576 | tf_op jit(solution)/shard_map/reshape | solution.py:332
  1.3 87.5 %decode_layer.1 = bf16[1,512]{1,0:T(2,128)(2,1)} custom-call(s32[16]{0:T(128)} %refs_0_.1, s32[16]{0:T(128)} %refs_1_.1, f32[32,1,128]{2,1,0:T(1,128)} %bitcast_convert_fusion.refs_2_, f32[32,1,128]{2,1,0:T(1,128)} %bitcast.11, f32[32,1,128]{2,1,0:T(1,128)} %bitcast.12, bf16[64,512]{1,0:T(8,128)(2,1)} %refs_5_.1, bf16[64,128]{1,0:T(8,128)(2,1)} %refs_6_.1, ...), custom_call_target="tpu_custom_call" | custom-call | tf_op jit(solution)/shard_map/decode_layer/pallas_call | solution.py:357
  88.8 1.3 %copy.16 = bf16[1,512]{1,0:T(2,128)(2,1)} copy(bf16[1,512]{1,0:T(2,128)(2,1)} %decode_layer.1) | data formatting | bytes 2048
